TPU v7x, 32 devices: a whole 2x2x4 slice. The times are simulated.
32 devices in a mesh: seg: 4 (over z), rank: 8 (over y, x, core).
Axes of the slice: x: 2, y: 2, z: 4, core: 2. Of those that a mesh axis runs over, the one named last changes fastest.
Arguments:
- children: float32 [20, 35, 65536], P(None, None, ('seg', 'rank')), may hold values from -6 to 6
- pair_order: int32 [32, 2048], P(('seg', 'rank')), may hold values from 0 to 2047, each once within a row
- rim_order: int32 [32, 256], P(('seg', 'rank')), may hold values from 0 to 255, each once within a row
- pair_type: int32 [32, 1024], P(('seg', 'rank')), may hold values from 0 to 2
- projection: float32 [3, 2, 35, 35], replicated, may hold values from -0.75 to 0.75
- new_owner: int32 [32, 1024], P(('seg', 'rank')), may hold values from 0 to 31, as said below
- new_slot: int32 [32, 1024], P(('seg', 'rank')), may hold values from 0 to 1023, as said below
Outputs:
- parents: float32 [20, 35, 32768], P(None, None, ('seg', 'rank'))
Inputs may be any that keep to these rules, and one draw needn't show every extreme that they name: `pair_order`: each row is a permutation. `rim_order`: each row is a permutation. `new_owner`: A device of seg g and rank r sends its parents to itself, to other devices of seg g, and to rank r of seg g + 1 (segments counted around); at most 64 to each other device of its seg, exactly 64 to rank r + 1 of seg g (ranks counted around), exactly 64 to seg g + 1; every device receives exactly 1024 parents. The pairs (new_owner, new_slot) are distinct over all parents.
All inputs are finite; a program needn't handle non-finite values.
Results may differ from a plain program's by a relative error of at most 0.0003.
Values sent between devices are 32-bit elements; how exact they have to be, the bound alone decides.
A program may use at most 192 MiB of HBM per device.

v0:
```python
import functools

import jax
import jax.numpy as jnp
from jax import lax
from jax.experimental import pallas as pl
from jax.experimental.pallas import tpu as pltpu
from jax.sharding import PartitionSpec as P

LANES = 128
SUB = 8
F32 = jnp.float32
BF16 = jnp.bfloat16
I32 = jnp.int32
MESH = pl.DeviceIdType.MESH


def row(i):
    return pl.ds(pl.multiple_of(i * SUB, SUB), SUB)


def split(x):
    high = x.astype(BF16)
    low = (x - high.astype(F32)).astype(BF16)
    return high, low


def column_of(line):
    return jnp.broadcast_to(line, (LANES, line.shape[1])).T


def fused_kernel(
    n_seg,
    n_rank,
    near_cap,
    far_cap,
    children,
    pair_s,
    rim_s,
    kind_v,
    owner_v,
    slot_v,
    weight,
    out,
    own,
    rim,
    stage,
    ext,
    first,
    second,
    leaving,
    landed,
    final,
    sent_slots,
    got_slots,
    index_v,
    index_s,
    source_v,
    source_s,
    kind_rows,
    column_a,
    column_b,
    column_c,
    own_sem,
    rim_sems,
    slot_send,
    slot_recv,
    near_send,
    near_recv,
    index_sem,
):
    fields, modes, child_count = children.shape
    rim_len = rim_s.shape[1]
    kept = child_count - rim_len
    parent_count = child_count // 2
    kinds = weight.shape[1] // LANES
    pitch = (modes + 7) // 8 * 8
    per_group = LANES // pitch
    groups = -(-fields // per_group)
    near_total = n_rank * near_cap
    spread = (n_rank + 1) * LANES
    my_seg = lax.axis_index("seg")
    my_rank = lax.axis_index("rank")
    me = my_seg * n_rank + my_rank
    count = n_seg * n_rank
    before = (me + count - 1) % count
    after = (me + 1) % count
    seg_up = (my_seg + 1) % n_seg
    seg_down = (my_seg + n_seg - 1) % n_seg

    got_slots[...] = jnp.full_like(got_slots, parent_count)
    barrier = pltpu.get_barrier_semaphore()

    def greet(seg, rank):
        pl.semaphore_signal(barrier, inc=1, device_id=(seg, rank), device_id_type=MESH)

    greet(before // n_rank, before % n_rank)
    greet(after // n_rank, after % n_rank)
    greet(seg_up, my_rank)
    greet(seg_down, my_rank)

    def greet_rank(k, carry):
        greet(my_seg, (my_rank + k) % n_rank)
        return carry

    lax.fori_loop(1, n_rank, greet_rank, 0)
    load_own = pltpu.make_async_copy(
        children.at[:, :, pl.ds(rim_len, kept)], own, own_sem
    )
    load_own.start()
    pl.semaphore_wait(barrier, n_rank + 3)
    send_rim = pltpu.make_async_remote_copy(
        src_ref=children.at[:, :, pl.ds(0, rim_len)],
        dst_ref=rim,
        send_sem=rim_sems.at[0],
        recv_sem=rim_sems.at[1],
        device_id=(before // n_rank, before % n_rank),
        device_id_type=MESH,
    )
    send_rim.start()

    ext_flat = ext.reshape(ext.shape[0] * SUB, LANES)
    leaving_flat = leaving.reshape(leaving.shape[0] * SUB, LANES)
    landed_flat = landed.reshape(landed.shape[0] * SUB, LANES)

    owner = owner_v[...]
    slot = slot_v[...]
    owner_seg = owner // n_rank
    owner_rank = owner - owner_seg * n_rank
    distant = owner_seg != my_seg
    staying = owner == me
    bin_of = jnp.where(distant, n_rank, jnp.where(staying, -1, owner_rank))
    columns_of(bin_of, column_a)
    under = lax.broadcasted_iota(I32, (parent_count, LANES), 0)
    lane = lax.broadcasted_iota(I32, (parent_count, LANES), 1)
    for c in range(parent_count // LANES):
        at = slice(c * LANES, (c + 1) * LANES)
        same = (column_a[...] == bin_of[:, at]) & (under < lane + c * LANES)
        place = jnp.sum(jnp.where(same, 1, 0), axis=0, keepdims=True)
        stays = bin_of[:, at] < 0
        leave = jnp.where(stays, slot[:, at] + spread, bin_of[:, at] * LANES + place)
        column_b[at, :] = column_of(leave)
        info = lax.broadcasted_iota(I32, (1, LANES), 1) + c * LANES
        info = info + slot[:, at] * 1024 + kind_v[:, at] * (1024 * 1024)
        column_c[at, :] = column_of(info)

    def lines(value):
        return jnp.broadcast_to(value, (SUB, LANES))

    def invert(c):
        hit = column_b[...] == lane + c * LANES
        return jnp.max(jnp.where(hit, column_c[...], -1), axis=0, keepdims=True)

    def plan(c):
        at = pl.ds(pl.multiple_of(c * LANES, LANES), LANES)
        got = invert(c)
        used = got >= 0
        got = jnp.maximum(got, 0)
        index_v[:, at] = lines(got % 1024)
        kind_rows[:, at] = lines(got // (1024 * 1024))
        return jnp.where(used, got // 1024 % 1024, parent_count)

    def leave_plan(c, carry):
        at = pl.ds(pl.multiple_of(c * LANES, LANES), LANES)
        sent_slots[:, at] = lines(plan(c))
        return carry

    lax.fori_loop(0, n_rank + 1, leave_plan, 0)

    def slot_copy(r, seg, rank, landing):
        return pltpu.make_async_remote_copy(
            src_ref=sent_slots.at[:, pl.ds(pl.multiple_of(r * LANES, LANES), LANES)],
            dst_ref=got_slots.at[:, pl.ds(pl.multiple_of(landing * LANES, LANES), LANES)],
            send_sem=slot_send.at[r],
            recv_sem=slot_recv.at[landing],
            device_id=(seg, rank),
            device_id_type=MESH,
        )

    def near_copy(r, landing):
        size = near_cap
        return pltpu.make_async_remote_copy(
            src_ref=leaving.at[pl.ds(r * size, size)],
            dst_ref=landed.at[pl.ds(parent_count + landing * size, size)],
            send_sem=near_send.at[r],
            recv_sem=near_recv.at[landing],
            device_id=(my_seg, r),
            device_id_type=MESH,
        )

    far_copy = pltpu.make_async_remote_copy(
        src_ref=leaving.at[pl.ds(near_total, far_cap)],
        dst_ref=landed.at[pl.ds(parent_count + near_total, far_cap)],
        send_sem=near_send.at[n_rank],
        recv_sem=near_recv.at[n_rank],
        device_id=(seg_up, my_rank),
        device_id_type=MESH,
    )

    greet_slots(n_rank, my_seg, my_rank, slot_copy)
    slot_copy(n_rank, seg_up, my_rank, n_rank).start()

    def home_plan(c, carry):
        plan(n_rank + 1 + c)
        return carry

    lax.fori_loop(0, parent_count // LANES, home_plan, 0)
    to_scalar = pltpu.make_async_copy(index_v, index_s, index_sem.at[0])
    to_scalar.start()

    stage[...] = jnp.zeros_like(stage)
    load_own.wait()

    def to_rows(part, size, base):
        for g in range(groups):
            for j in range(per_group):
                f = g * per_group + j
                if f < fields:
                    stage[pitch * j : pitch * j + modes, 0:size] = part[f]

            def turn(c, carry, g=g):
                block = stage[:, pl.ds(pl.multiple_of(c * LANES, LANES), LANES)]
                ext_flat[pl.ds((base + c * LANES) * SUB + g, LANES, stride=SUB), :] = block.T
                return carry

            lax.fori_loop(0, size // LANES, turn, 0, unroll=2)

    to_rows(own, kept, 0)
    w_high, w_low = split(weight[...])
    w_both = jnp.concatenate([w_high, w_low], axis=1)
    wide = kinds * LANES
    to_scalar.wait()
    send_rim.wait()
    to_rows(rim, rim_len, child_count)

    def border(e, carry):
        ext[kept + e] = ext[child_count + rim_s[0, e]]
        return carry

    lax.fori_loop(0, rim_len, border, 0, unroll=8)

    def pick(at, base, size):
        def step(i, carry):
            q = index_s[0, at + i]
            a = pair_s[0, 2 * q]
            b = pair_s[0, 2 * q + 1]
            first[row(base + i), :] = ext[a]
            second[row(base + i), :] = ext[b]
            return carry

        lax.fori_loop(0, size, step, 0, unroll=8)

    def project(kind, size, into, base):
        parts = []
        for g in range(groups):
            at = pl.ds(g, size, stride=SUB)
            parts.append(jnp.concatenate([first[at, :], second[at, :]], axis=1))
        high, low = split(jnp.concatenate(parts, axis=0))
        both = jnp.dot(high, w_both, preferred_element_type=F32)
        total = both[:, :wide] + both[:, wide:]
        total = total + jnp.dot(low, w_high, preferred_element_type=F32)
        for g in range(groups):
            mine = total[g * size : (g + 1) * size]
            chosen = mine[:, :LANES]
            for t in range(1, kinds):
                chosen = jnp.where(kind == t, mine[:, t * LANES : (t + 1) * LANES], chosen)
            into[pl.ds(base * SUB + g, size, stride=SUB), :] = chosen

    def kind_of(c, size):
        at = pl.ds(pl.multiple_of(c * LANES, LANES), LANES)
        return column_of(kind_rows[0:1, at])[:size]

    pick(n_rank * LANES, 0, far_cap)
    project(kind_of(n_rank, far_cap), far_cap, leaving_flat, near_total)
    far_copy.start()
    together = min(LANES // near_cap, n_rank)

    def near_step(n, carry):
        kind = []
        for k in range(together):
            r = n * together + k
            pick(r * LANES, k * near_cap, near_cap)
            kind.append(kind_of(r, near_cap))
        size = together * near_cap
        project(jnp.concatenate(kind, axis=0), size, leaving_flat, n * size)
        for k in range(together):
            r = n * together + k

            @pl.when(r != my_rank)
            def _(r=r):
                near_copy(r, my_rank).start()

        return carry

    lax.fori_loop(0, n_rank // together, near_step, 0)

    def home_step(c, carry):
        pick(spread + c * LANES, 0, LANES)
        project(kind_of(n_rank + 1 + c, LANES), LANES, landed_flat, c * LANES)
        return carry

    lax.fori_loop(0, parent_count // LANES, home_step, 0)

    def slots_done(k, carry):
        r = (my_rank + k) % n_rank
        slot_copy(r, my_seg, r, r).wait()
        return carry

    lax.fori_loop(1, n_rank, slots_done, 0)
    slot_copy(n_rank, seg_up, my_rank, n_rank).wait()
    for r in range(n_rank + 1):
        size = far_cap if r == n_rank else near_cap
        tile = column_of(got_slots[0:1, r * LANES : (r + 1) * LANES])
        column_b[r * near_cap : r * near_cap + size, :] = tile[:size]
    arrivals = near_total + far_cap
    arrived = lax.broadcasted_iota(I32, (arrivals, LANES), 0) + parent_count
    slot_lane = lax.broadcasted_iota(I32, (arrivals, LANES), 1)
    for c in range(parent_count // LANES):
        hit = column_b[0:arrivals, :] == slot_lane + c * LANES
        found = jnp.max(jnp.where(hit, arrived, -1), axis=0, keepdims=True)
        own_row = c * LANES + lax.broadcasted_iota(I32, (1, LANES), 1)
        source_v[:, c * LANES : (c + 1) * LANES] = lines(
            jnp.where(found >= 0, found, own_row)
        )
    to_source = pltpu.make_async_copy(source_v, source_s, index_sem.at[1])
    to_source.start()
    to_source.wait()

    def near_done(k, carry):
        r = (my_rank + k) % n_rank
        near_copy(r, r).wait()
        return carry

    lax.fori_loop(1, n_rank, near_done, 0)
    far_copy.wait()

    def gather(s, carry):
        final[row(s), :] = landed[source_s[0, s]]
        return carry

    lax.fori_loop(0, parent_count, gather, 0, unroll=8)

    def back(c, carry):
        lanes = pl.ds(pl.multiple_of(c * LANES, LANES), LANES)
        for g in range(groups):
            tile = final[pl.ds(c * LANES * SUB + g, LANES, stride=SUB), :].T
            for j in range(per_group):
                f = g * per_group + j
                if f < fields:
                    out[f, :, lanes] = tile[pitch * j : pitch * j + modes]
        return carry

    lax.fori_loop(0, parent_count // LANES, back, 0)


def columns_of(line, ref):
    for c in range(line.shape[1] // LANES):
        at = slice(c * LANES, (c + 1) * LANES)
        ref[at, :] = column_of(line[:, at])


def greet_slots(n_rank, my_seg, my_rank, slot_copy):
    def send(k, carry):
        r = (my_rank + k) % n_rank
        slot_copy(r, my_seg, r, my_rank).start()
        return carry

    lax.fori_loop(1, n_rank, send, 0)


def wide_weights(projection):
    kinds, _, modes, _ = projection.shape
    pitch = (modes + 7) // 8 * 8
    per_group = LANES // pitch
    small = jnp.pad(projection, ((0, 0), (0, 0), (0, pitch - modes), (0, pitch - modes)))
    small = jnp.transpose(small, (1, 3, 0, 2))
    tiled = jnp.tile(small, (1, per_group, 1, per_group))
    at = jnp.arange(per_group * pitch, dtype=I32) // pitch
    tiled = jnp.where((at[:, None] == at[None, :])[None, :, None, :], tiled, 0.0)
    left = LANES - per_group * pitch
    tiled = jnp.pad(tiled, ((0, 0), (0, left), (0, 0), (0, left)))
    return tiled.reshape(2 * LANES, kinds * LANES)


def per_device(children, pair_order, rim_order, pair_type, projection, new_owner, new_slot):
    fields, modes, child_count = children.shape
    rim_len = rim_order.shape[1]
    parent_count = child_count // 2
    n_rank = lax.axis_size("rank")
    n_seg = lax.axis_size("seg")
    near_cap = parent_count // (2 * n_rank)
    far_cap = parent_count // 16
    near_total = n_rank * near_cap
    spread = (n_rank + 1) * LANES
    weight = wide_weights(projection)
    vmem = pl.BlockSpec(memory_space=pltpu.VMEM)
    smem = pl.BlockSpec(memory_space=pltpu.SMEM)
    hbm = pl.BlockSpec(memory_space=pl.ANY)
    dma = pltpu.SemaphoreType.DMA
    return pl.pallas_call(
        functools.partial(fused_kernel, n_seg, n_rank, near_cap, far_cap),
        out_shape=jax.ShapeDtypeStruct((fields, modes, parent_count), F32),
        in_specs=[hbm, smem, smem, vmem, vmem, vmem, vmem],
        out_specs=vmem,
        scratch_shapes=[
            pltpu.VMEM((fields, modes, child_count - rim_len), F32),
            pltpu.VMEM((fields, modes, rim_len), F32),
            pltpu.VMEM((LANES, child_count), F32),
            pltpu.VMEM((child_count + rim_len, SUB, LANES), F32),
            pltpu.VMEM((LANES * SUB, LANES), F32),
            pltpu.VMEM((LANES * SUB, LANES), F32),
            pltpu.VMEM((near_total + far_cap, SUB, LANES), F32),
            pltpu.VMEM((parent_count + near_total + far_cap, SUB, LANES), F32),
            pltpu.VMEM((parent_count * SUB, LANES), F32),
            pltpu.VMEM((SUB, spread), I32),
            pltpu.VMEM((SUB, spread), I32),
            pltpu.VMEM((SUB, spread + parent_count), I32),
            pltpu.SMEM((SUB, spread + parent_count), I32),
            pltpu.VMEM((SUB, parent_count), I32),
            pltpu.SMEM((SUB, parent_count), I32),
            pltpu.VMEM((SUB, spread + parent_count), I32),
            pltpu.VMEM((parent_count, LANES), I32),
            pltpu.VMEM((parent_count, LANES), I32),
            pltpu.VMEM((parent_count, LANES), I32),
            dma,
            dma((2,)),
            dma((n_rank + 1,)),
            dma((n_rank + 1,)),
            dma((n_rank + 1,)),
            dma((n_rank + 1,)),
            dma((2,)),
        ],
        compiler_params=pltpu.CompilerParams(
            vmem_limit_bytes=58 * 1024 * 1024, collective_id=0, has_side_effects=True
        ),
        name="coarsen",
    )(children, pair_order, rim_order, pair_type, new_owner, new_slot, weight)


def solution(mesh):
    by_device = P(("seg", "rank"), None)
    in_specs = (
        P(None, None, ("seg", "rank")),
        by_device,
        by_device,
        by_device,
        P(),
        by_device,
        by_device,
    )
    out_specs = P(None, None, ("seg", "rank"))
    return jax.shard_map(
        per_device, mesh=mesh, in_specs=in_specs, out_specs=out_specs, check_vma=False
    )
```

profile of v0, /device:TPU:1, one launch (start us, length us, event | category | flops | bytes accessed | tf_op | source)
XLA Modules:
  0.0 60.2 jit_solution(128734925663167878)
XLA Ops:
  0.0 0.1 broadcast_compare_fusion
  0.1 1.0 %pad_bitcast_fusion = f32[2,40,3,40]{1,0,3,2:T(2,128)S(1)} fusion(f32[3,2,35,35]{3,1,2,0:T(2,128)} %param.11), kind=kLoop, calls=%fused_computation.2 | loop fusion | bytes 67800 | tf_op jit(solution)/shard_map/transpose | solution.py:376
  1.1 0.1 copy.9
  1.2 0.3 tile.4
  1.5 0.5 tile.10
  2.1 0.1 copy.14
  2.2 0.1 pad.9.clone
  2.3 0.8 %copy.17 = f32[32,8,3,128]{3,1,2,0:T(8,128)} copy(f32[32,8,3,128]{3,2,1,0:T(4,128)S(1)} %bitcast.9) | data formatting | bytes 786432
  3.1 53.1 %coarsen.1 = f32[20,35,1024]{2,1,0:T(8,128)} custom-call(f32[20,35,2048]{2,1,0:T(8,128)} %children.1, s32[1,2048]{1,0:T(1,128)} %pair_s.1, s32[1,256]{1,0:T(1,128)} %rim_s.1, s32[1,1024]{1,0:T(1,128)} %kind_v.1, s32[1,1024]{1,0:T(1,128)} %owner_v.1, s32[1,1024]{1,0:T(1,128)} %slot_v.1, f32[256,384]{1,0:T(8,128)} %bitcast.10), custom_call_target="tpu_custom_call" | custom-call | tf_op jit(solution)/shard_map/coarsen/pallas_call | solution.py:400
  56.2 4.1 %copy.19 = f32[20,35,1024]{2,1,0:T(8,128)} copy(f32[20,35,1024]{2,1,0:T(8,128)} %coarsen.1) | data formatting | bytes 5734400
  (2 shorter events, 0.0 us)
where the time goes:
time: 60.9 us; the launch traced here: 60.2 us
  Pallas kernels  53.1 us (87%)
  local copies, waits for them, and re-layouts  6.96 us (11%)
    pallas_call x1, Pallas kernels, per_device(): pl.pallas_call(functools.partial(fused_kernel, n_seg, n_rank, near_cap, f...  53.1 us
    unnamed x3, local copies, waits for them, and re-layouts  4.98 us

commit v1 on v0

--- a/solution.py
+++ b/solution.py
@@ -40,7 +40,7 @@
     kind_v,
     owner_v,
     slot_v,
-    weight,
+    projection,
     out,
     own,
     rim,
@@ -61,6 +61,7 @@
     column_a,
     column_b,
     column_c,
+    weight,
     own_sem,
     rim_sems,
     slot_send,
@@ -73,7 +74,7 @@
     rim_len = rim_s.shape[1]
     kept = child_count - rim_len
     parent_count = child_count // 2
-    kinds = weight.shape[1] // LANES
+    kinds = projection.shape[0]
     pitch = (modes + 7) // 8 * 8
     per_group = LANES // pitch
     groups = -(-fields // per_group)
@@ -180,8 +181,8 @@
     def near_copy(r, landing):
         size = near_cap
         return pltpu.make_async_remote_copy(
-            src_ref=leaving.at[pl.ds(r * size, size)],
-            dst_ref=landed.at[pl.ds(parent_count + landing * size, size)],
+            src_ref=leaving.at[pl.ds(r * size, size), pl.ds(0, groups)],
+            dst_ref=landed.at[pl.ds(parent_count + landing * size, size), pl.ds(0, groups)],
             send_sem=near_send.at[r],
             recv_sem=near_recv.at[landing],
             device_id=(my_seg, r),
@@ -189,8 +190,8 @@
         )
 
     far_copy = pltpu.make_async_remote_copy(
-        src_ref=leaving.at[pl.ds(near_total, far_cap)],
-        dst_ref=landed.at[pl.ds(parent_count + near_total, far_cap)],
+        src_ref=leaving.at[pl.ds(near_total, far_cap), pl.ds(0, groups)],
+        dst_ref=landed.at[pl.ds(parent_count + near_total, far_cap), pl.ds(0, groups)],
         send_sem=near_send.at[n_rank],
         recv_sem=near_recv.at[n_rank],
         device_id=(seg_up, my_rank),
@@ -226,6 +227,31 @@
             lax.fori_loop(0, size // LANES, turn, 0, unroll=2)
 
     to_rows(own, kept, 0)
+    wide_at = lax.broadcasted_iota(I32, (LANES, modes), 0)
+    mode_at = lax.broadcasted_iota(I32, (LANES, modes), 1)
+    inside = wide_at < per_group * pitch
+    spread_modes = jnp.where((wide_at % pitch == mode_at) & inside, 1.0, 0.0)
+    block_a = lax.broadcasted_iota(I32, (LANES, LANES), 0) // pitch
+    block_b = lax.broadcasted_iota(I32, (LANES, LANES), 1) // pitch
+    for t in range(kinds):
+        for child in range(2):
+            tall = lax.dot_general(
+                spread_modes,
+                projection[t, child],
+                (((1,), (1,)), ((), ())),
+                precision=lax.Precision.HIGHEST,
+                preferred_element_type=F32,
+            )
+            full = lax.dot_general(
+                tall,
+                spread_modes,
+                (((1,), (1,)), ((), ())),
+                precision=lax.Precision.HIGHEST,
+                preferred_element_type=F32,
+            )
+            weight[child * LANES : (child + 1) * LANES, t * LANES : (t + 1) * LANES] = (
+                jnp.where(block_a == block_b, full, 0.0)
+            )
     w_high, w_low = split(weight[...])
     w_both = jnp.concatenate([w_high, w_low], axis=1)
     wide = kinds * LANES
@@ -275,7 +301,10 @@
     far_copy.start()
     together = min(LANES // near_cap, n_rank)
 
-    def near_step(n, carry):
+    chunks = n_rank // together
+
+    def near_step(k, carry):
+        n = (my_rank // together + 1 + k) % chunks
         kind = []
         for k in range(together):
             r = n * together + k
@@ -292,7 +321,7 @@
 
         return carry
 
-    lax.fori_loop(0, n_rank // together, near_step, 0)
+    lax.fori_loop(0, chunks, near_step, 0)
 
     def home_step(c, carry):
         pick(spread + c * LANES, 0, LANES)
@@ -368,20 +397,6 @@
     lax.fori_loop(1, n_rank, send, 0)
 
 
-def wide_weights(projection):
-    kinds, _, modes, _ = projection.shape
-    pitch = (modes + 7) // 8 * 8
-    per_group = LANES // pitch
-    small = jnp.pad(projection, ((0, 0), (0, 0), (0, pitch - modes), (0, pitch - modes)))
-    small = jnp.transpose(small, (1, 3, 0, 2))
-    tiled = jnp.tile(small, (1, per_group, 1, per_group))
-    at = jnp.arange(per_group * pitch, dtype=I32) // pitch
-    tiled = jnp.where((at[:, None] == at[None, :])[None, :, None, :], tiled, 0.0)
-    left = LANES - per_group * pitch
-    tiled = jnp.pad(tiled, ((0, 0), (0, left), (0, 0), (0, left)))
-    return tiled.reshape(2 * LANES, kinds * LANES)
-
-
 def per_device(children, pair_order, rim_order, pair_type, projection, new_owner, new_slot):
     fields, modes, child_count = children.shape
     rim_len = rim_order.shape[1]
@@ -392,7 +407,7 @@
     far_cap = parent_count // 16
     near_total = n_rank * near_cap
     spread = (n_rank + 1) * LANES
-    weight = wide_weights(projection)
+    kinds = projection.shape[0]
     vmem = pl.BlockSpec(memory_space=pltpu.VMEM)
     smem = pl.BlockSpec(memory_space=pltpu.SMEM)
     hbm = pl.BlockSpec(memory_space=pl.ANY)
@@ -422,6 +437,7 @@
             pltpu.VMEM((parent_count, LANES), I32),
             pltpu.VMEM((parent_count, LANES), I32),
             pltpu.VMEM((parent_count, LANES), I32),
+            pltpu.VMEM((2 * LANES, kinds * LANES), F32),
             dma,
             dma((2,)),
             dma((n_rank + 1,)),
@@ -434,7 +450,7 @@
             vmem_limit_bytes=58 * 1024 * 1024, collective_id=0, has_side_effects=True
         ),
         name="coarsen",
-    )(children, pair_order, rim_order, pair_type, new_owner, new_slot, weight)
+    )(children, pair_order, rim_order, pair_type, new_owner, new_slot, projection)
 
 
 def solution(mesh):

time: 60.9 us -> 54.7 us (0.90)
  Pallas kernels: 53.1 us -> 48.9 us
  local copies, waits for them, and re-layouts: 6.96 us -> 5.62 us
    pallas_call x1, Pallas kernels: 53.1 us -> 48.9 us  [per_device(): pl.pallas_call(functools.partial(fused_kernel, n_seg, n_rank, near_cap, f...]
    transpose x2 -> x0, local copies, waits for them, and re-layouts: 1.05 us -> none  [wide_weights(): small = jnp.transpose(small, (1, 3, 0, 2))]
    another operation x2 -> x0, local copies, waits for them, and re-layouts: 0.84 us -> none  [wide_weights(): tiled = jnp.tile(small, (1, per_group, 1, per_group))]
    unnamed x3 -> x2, local copies, waits for them, and re-layouts: 4.98 us -> 5.62 us
where the time goes in v1:
time: 54.7 us; the launch traced here: 54.5 us
  Pallas kernels  48.9 us (89%)
  local copies, waits for them, and re-layouts  5.62 us (10%)
    pallas_call x1, Pallas kernels, per_device(): pl.pallas_call(functools.partial(fused_kernel, n_seg, n_rank, near_cap, f...  48.9 us
    unnamed x2, local copies, waits for them, and re-layouts  5.62 us

profile of v1, /device:TPU:1, one launch (start us, length us, event | category | flops | bytes accessed | tf_op | source)
XLA Modules:
  0.0 54.5 jit_solution(3162573610664564825)
XLA Ops:
  0.0 1.6 %copy.8.projection = f32[3,2,35,35]{3,2,1,0:T(8,128)} copy(f32[3,2,35,35]{3,1,2,0:T(2,128)} %param.11) | data formatting | bytes 58800 | tf_op args[4]
  1.6 48.9 %coarsen.1 = f32[20,35,1024]{2,1,0:T(8,128)} custom-call(f32[20,35,2048]{2,1,0:T(8,128)} %children.1, s32[1,2048]{1,0:T(1,128)} %pair_s.1, s32[1,256]{1,0:T(1,128)} %rim_s.1, s32[1,1024]{1,0:T(1,128)} %kind_v.1, s32[1,1024]{1,0:T(1,128)} %owner_v.1, s32[1,1024]{1,0:T(1,128)} %slot_v.1, f32[3,2,35,35]{3,2,1,0:T(8,128)} %copy.8.projection), custom_call_target="tpu_custom_call" | custom-call | tf_op jit(solution)/shard_map/coarsen/pallas_call | solution.py:415
  50.5 4.1 %copy.10 = f32[20,35,1024]{2,1,0:T(8,128)} copy(f32[20,35,1024]{2,1,0:T(8,128)} %coarsen.1) | data formatting | bytes 5734400

commit v2 on v1

--- a/solution.py
+++ b/solution.py
@@ -224,7 +224,7 @@
                 ext_flat[pl.ds((base + c * LANES) * SUB + g, LANES, stride=SUB), :] = block.T
                 return carry
 
-            lax.fori_loop(0, size // LANES, turn, 0, unroll=2)
+            lax.fori_loop(0, size // LANES, turn, 0, unroll=min(7, size // LANES))
 
     to_rows(own, kept, 0)
     wide_at = lax.broadcasted_iota(I32, (LANES, modes), 0)
@@ -274,7 +274,7 @@
             second[row(base + i), :] = ext[b]
             return carry
 
-        lax.fori_loop(0, size, step, 0, unroll=8)
+        lax.fori_loop(0, size, step, 0, unroll=16)
 
     def project(kind, size, into, base):
         parts = []
@@ -367,7 +367,7 @@
         final[row(s), :] = landed[source_s[0, s]]
         return carry
 
-    lax.fori_loop(0, parent_count, gather, 0, unroll=8)
+    lax.fori_loop(0, parent_count, gather, 0, unroll=16)
 
     def back(c, carry):
         lanes = pl.ds(pl.multiple_of(c * LANES, LANES), LANES)

time: 54.7 us -> 54.3 us (level)
  no operation moved by 1% of the time
where the time goes in v2:
time: 54.3 us; the launch traced here: 54.1 us
  Pallas kernels  48.5 us (89%)
  local copies, waits for them, and re-layouts  5.62 us (10%)
    pallas_call x1, Pallas kernels, per_device(): pl.pallas_call(functools.partial(fused_kernel, n_seg, n_rank, near_cap, f...  48.5 us
    unnamed x2, local copies, waits for them, and re-layouts  5.62 us

profile of v2, /device:TPU:1, one launch (start us, length us, event | category | flops | bytes accessed | tf_op | source)
XLA Modules:
  0.0 54.1 jit_solution(12244907284556997964)
XLA Ops:
  0.0 1.6 %copy.8.projection = f32[3,2,35,35]{3,2,1,0:T(8,128)} copy(f32[3,2,35,35]{3,1,2,0:T(2,128)} %param.11) | data formatting | bytes 58800 | tf_op args[4]
  1.6 48.5 %coarsen.1 = f32[20,35,1024]{2,1,0:T(8,128)} custom-call(f32[20,35,2048]{2,1,0:T(8,128)} %children.1, s32[1,2048]{1,0:T(1,128)} %pair_s.1, s32[1,256]{1,0:T(1,128)} %rim_s.1, s32[1,1024]{1,0:T(1,128)} %kind_v.1, s32[1,1024]{1,0:T(1,128)} %owner_v.1, s32[1,1024]{1,0:T(1,128)} %slot_v.1, f32[3,2,35,35]{3,2,1,0:T(8,128)} %copy.8.projection), custom_call_target="tpu_custom_call" | custom-call | tf_op jit(solution)/shard_map/coarsen/pallas_call | solution.py:415
  50.1 4.1 %copy.10 = f32[20,35,1024]{2,1,0:T(8,128)} copy(f32[20,35,1024]{2,1,0:T(8,128)} %coarsen.1) | data formatting | bytes 5734400
